TPU v7x, 256 devices: a whole 4x4x8 slice. The times are simulated.
256 devices in a mesh: ctx: 128 (over x_lo, y, z, core), tp: 2 (over x_hi).
Axes of the slice: x: 4 (x_hi: 2, x_lo: 2; x = x_hi * 2 + x_lo), y: 4, z: 8, core: 2. Of those that a mesh axis runs over, the one named last changes fastest.
Arguments:
- queries: bfloat16 [32768, 2048], P('ctx', 'tp'), may hold values from -5 to 5
- keys: bfloat16 [32768, 256], P('ctx', 'tp'), may hold values from -5 to 5
- values: bfloat16 [32768, 256], P('ctx', 'tp'), may hold values from -6 to 6
- out_weight: bfloat16 [2048, 4096], P('tp'), may hold values from -0.125 to 0.125
- cotangent: bfloat16 [32768, 4096], P('ctx', 'tp'), may hold values from -6 to 6
- doc_lengths: int32 [64], replicated, may hold values from 1 to 2048, 32768 in all
Outputs:
- mixed_out: bfloat16 [32768, 4096], P('ctx', 'tp')
- query_grad: bfloat16 [32768, 2048], P('ctx', 'tp')
- keys_gradient: bfloat16 [32768, 256], P('ctx', 'tp')
- values_gradient: bfloat16 [32768, 256], P('ctx', 'tp')
Inputs may be any that keep to these rules, and one draw needn't show every extreme that they name: `doc_lengths`: document lengths in order along the packed sequence; they sum to 32768 and the longest is exactly 2048.
All inputs are finite; a program needn't handle non-finite values.
Results may differ from a plain program's by a relative error of at most 0.022.
Values may be sent and summed in bfloat16 or wider, within the bound.
A program may use at most 192 MiB of HBM per device.

v0:
```python
from functools import partial
import math

import jax
import jax.numpy as jnp
from jax import lax
from jax.experimental import pallas as pl
from jax.experimental.pallas import tpu as pltpu
from jax.sharding import PartitionSpec as P

HEAD_WIDTH = 128
HOPS = 4
CHUNKS = 4
NEG = -1e30
MESH = pl.DeviceIdType.MESH
F32 = jnp.float32
BF16 = jnp.bfloat16


def mm(a, b):
    return jnp.dot(a, b, preferred_element_type=F32)


def mm_nt(a, b):
    return lax.dot_general(a, b, (((1,), (1,)), ((), ())), preferred_element_type=F32)


def kernel(
    ctx_size,
    q_hbm, k_hbm, v_hbm, w_hbm, cot_hbm, lens_ref,
    out_hbm, dq_hbm, dk_hbm, dv_hbm,
    q_s, q_t, kv, k_t, v_t, w_v, cot, exps, bias, o_t, o_low, attn,
    row_max, row_sum, stage_max, delta, ga_t, do_t, do_s, dq_t, dkv,
    part_send, part_recv, run_send, run_recv, relay, rs_send, rs_recv, own_out, dq_out, dkv_out,
    load_sem, w_sem, out_sem,
    hop_send, hop_recv, chip_send, chip_recv,
    x_send, x_recv, y_send, y_recv,
    part_ss, part_rs, run_ss, run_rs,
):
    heads, tok, width = q_s.shape
    cols = own_out.shape[2]
    half = CHUNKS * cols
    me = lax.axis_index("ctx")
    tp = lax.axis_index("tp")
    core = lax.rem(me, 2)
    chip = me // 2
    chips = ctx_size // 2
    nxt = lax.rem(chip + 1, chips) * 2 + core
    prv = lax.rem(chip + chips - 1, chips) * 2 + core
    mate = me + 1 - 2 * core
    across = lax.rem(me + ctx_size // 2, ctx_size)
    score_scale = 1.0 / math.sqrt(HEAD_WIDTH)
    log2_scale = score_scale / math.log(2.0)

    def on(ctx_id, tp_id):
        return {"ctx": ctx_id, "tp": tp_id}

    kv_loads = [
        pltpu.make_async_copy(k_hbm, kv.at[0, 0], load_sem.at[0]),
        pltpu.make_async_copy(v_hbm, kv.at[0, 1], load_sem.at[1]),
    ]
    q_loads = [
        pltpu.make_async_copy(q_hbm.at[:, pl.ds(h * width, width)], q_s.at[h], load_sem.at[2 + h])
        for h in range(heads)
    ]
    cot_loads = [
        pltpu.make_async_copy(cot_hbm.at[:, pl.ds(c * cols, cols)], cot.at[0, c], load_sem.at[2 + heads + c])
        for c in range(CHUNKS)
    ]
    w_loads = [
        pltpu.make_async_copy(
            w_hbm.at[:, pl.ds(pl.multiple_of(side * half, half), half)], w_v.at[s], w_sem.at[s]
        )
        for s, side in ((0, tp), (1, 1 - tp))
    ]
    for copy in kv_loads + q_loads:
        copy.start()

    barrier = pltpu.get_barrier_semaphore()
    friends = [(nxt, tp), (prv, tp), (mate, tp), (across, tp), (across, 1 - tp)]
    for friend in friends:
        pl.semaphore_signal(barrier, inc=1, device_id=on(*friend), device_id_type=MESH)
    pl.semaphore_wait(barrier, len(friends))

    def hop(j, i):
        src = (k_hbm if i == 0 else v_hbm) if j == 1 else kv.at[2 * (j - 1), i]
        return pltpu.make_async_remote_copy(
            src_ref=src, dst_ref=kv.at[2 * j, i],
            send_sem=hop_send.at[j - 1, i], recv_sem=hop_recv.at[j - 1, i],
            device_id=on(nxt, tp), device_id_type=MESH,
        )

    def to_mate(j, i):
        turn = j - core
        return pltpu.make_async_remote_copy(
            src_ref=kv.at[2 * j, i], dst_ref=kv.at[2 * turn + 1, i],
            send_sem=chip_send.at[turn, i], recv_sem=chip_recv.at[turn, i],
            device_id=on(mate, tp), device_id_type=MESH,
        )

    def from_mate(j, i):
        return pltpu.make_async_remote_copy(
            src_ref=kv.at[2 * (j - 1), i], dst_ref=kv.at[2 * j - 1, i],
            send_sem=chip_send.at[j - 1, i], recv_sem=chip_recv.at[j - 1, i],
            device_id=on(mate, tp), device_id_type=MESH,
        )

    def forward_hop(j):
        for i in range(2):
            if j > 0:
                hop(j, i).wait_recv()
            if j < HOPS:
                hop(j + 1, i).start()
            if j == 0:
                @pl.when(core == 0)
                def _():
                    kv_loads[i].wait()
                    to_mate(j, i).start()

                @pl.when(core == 1)
                def _():
                    kv_loads[i].wait()
            elif j == HOPS:
                @pl.when(core == 1)
                def _():
                    to_mate(j, i).start()
            else:
                to_mate(j, i).start()

    def x_own(ph, c, src):
        way, i = c // 2, c % 2
        return pltpu.make_async_remote_copy(
            src_ref=src, dst_ref=relay.at[ph, way, i],
            send_sem=x_send.at[ph, way, i], recv_sem=x_recv.at[ph, way, i],
            device_id=on(across, tp if way == 0 else 1 - tp), device_id_type=MESH,
        )

    def x_pass(ph, way, i):
        c = 2 * way + i
        dst = cot.at[1, c] if ph == 0 else rs_recv.at[c]
        return pltpu.make_async_remote_copy(
            src_ref=relay.at[ph, way, i], dst_ref=dst,
            send_sem=y_send.at[ph, way, i], recv_sem=y_recv.at[ph, way, i],
            device_id=on(across, 1 - tp if way == 0 else tp), device_id_type=MESH,
        )

    def own_src(ph, c):
        return cot_hbm.at[:, pl.ds(c * cols, cols)] if ph == 0 else rs_send.at[c]

    def pass_on(ph, i):
        for way in range(2):
            x_own(ph, 2 * way + i, own_src(ph, 2 * way + i)).wait_recv()
            x_pass(ph, way, i).start()

    forward_hop(0)
    for c in (0, 2, 1, 3):
        x_own(0, c, own_src(0, c)).start()
    for copy in cot_loads + w_loads:
        copy.start()

    docs = lens_ref.shape[1]
    lens = jnp.broadcast_to(lens_ref[...].astype(F32), (docs, docs))
    before = lax.broadcasted_iota(jnp.int32, (docs, docs), 1) < lax.broadcasted_iota(
        jnp.int32, (docs, docs), 0
    )
    doc_start = jnp.sum(jnp.where(before, lens, 0.0), axis=1, keepdims=True)
    first = (me * tok).astype(F32)
    pos = lax.broadcasted_iota(jnp.int32, (1, tok), 1).astype(F32) + first
    start = jnp.max(jnp.where(doc_start <= pos, doc_start, 0.0), axis=0, keepdims=True) - first
    key_row = lax.broadcasted_iota(jnp.int32, (tok, tok), 0)
    query_col = lax.broadcasted_iota(jnp.int32, (tok, tok), 1)

    def set_bias(slot, d):
        allowed = key_row.astype(F32) >= start + float(d * tok)
        if d == 0:
            allowed = allowed & (key_row <= query_col)
        bias[slot] = jnp.where(allowed, 0.0, NEG)

    def turn_block(d):
        k_t[d] = kv[d, 0].T
        v_t[d] = kv[d, 1].T

    def fwd_stage(stage, blocks):
        for slot, d in enumerate(blocks):
            turn_block(d)
            set_bias(slot, d)

        def head(h, _):
            scores = [mm(kv[d, 0], q_t[h]) * log2_scale + bias[slot] for slot, d in enumerate(blocks)]
            top = scores[0] if len(scores) == 1 else jnp.maximum(scores[0], scores[1])
            top = jnp.max(top, axis=0, keepdims=True)
            if stage > 0:
                top = jnp.maximum(row_max[h], top)
            mass = None
            acc = None
            for d, s in zip(blocks, scores):
                e = jnp.exp2(s - top)
                exps[d, h] = e
                mass = e if mass is None else mass + e
                term = mm(v_t[d], e.astype(BF16))
                acc = term if acc is None else acc + term
            mass = jnp.sum(mass, axis=0, keepdims=True)
            if stage > 0:
                shrink = jnp.exp2(row_max[h] - top)
                mass = mass + row_sum[h] * shrink
                acc = acc + o_t[h] * shrink
            row_max[h] = top
            row_sum[h] = mass
            stage_max[stage, h] = top
            o_t[h] = acc
            return 0

        lax.fori_loop(0, heads, head, 0, unroll=2)

    def grad_half(s):
        def rows(r, _):
            at = pl.ds(pl.multiple_of(r * 2 * width, 2 * width), 2 * width)
            acc = ga_t[at] if s else None
            for c in range(CHUNKS):
                term = mm_nt(w_v[s, at, c * cols : (c + 1) * cols], cot[s, c])
                acc = term if acc is None else acc + term
            ga_t[at] = acc
            return 0

        lax.fori_loop(0, heads // 2, rows, 0)

    for copy in q_loads:
        copy.wait()
    for h in range(heads):
        q_t[h] = q_s[h].T
    fwd_stage(0, [0])
    for copy in cot_loads:
        copy.wait()
    w_loads[0].wait()
    grad_half(0)
    for j in range(1, HOPS + 1):
        forward_hop(j)
        for i in range(2):
            from_mate(j, i).wait_recv()
        fwd_stage(j, [2 * j - 1, 2 * j])
        if j == 2:
            pass_on(0, 0)
        if j == 4:
            pass_on(0, 1)

    for h in range(heads):
        inverse = 1.0 / row_sum[h]
        low = (o_t[h] * inverse).astype(BF16)
        o_low[h] = low
        attn[:, h * width : (h + 1) * width] = low.T
        for stage in range(HOPS + 1):
            stage_max[stage, h] = jnp.exp2(stage_max[stage, h] - row_max[h]) * inverse
    w_loads[1].wait()
    for c in (0, 2, 1, 3):
        rs_send[c] = mm(attn[...], w_v[1, :, c * cols : (c + 1) * cols]).astype(BF16)
        x_own(1, c, rs_send.at[c]).start()

    for way in range(2):
        for i in range(2):
            x_pass(0, way, i).wait_recv()
    grad_half(1)
    for h in range(heads):
        low = ga_t[h * width : (h + 1) * width].astype(BF16)
        do_t[h] = low
        do_s[h] = low.T
        delta[h] = jnp.sum(low.astype(F32) * o_low[h].astype(F32), axis=0, keepdims=True)

    def bwd_block(stage, d, first_block):
        dkv[...] = jnp.zeros_like(dkv)

        def head(h, _):
            prob = exps[d, h] * stage_max[stage, h]
            grad = prob * (mm(kv[d, 1], do_t[h]) - delta[h])
            prob = prob.astype(BF16)
            grad = grad.astype(BF16)
            dkv[1] += mm(prob, do_s[h])
            dkv[0] += mm(grad, q_s[h])
            term = mm(k_t[d], grad)
            dq_t[h] = term if first_block else dq_t[h] + term
            return 0

        lax.fori_loop(0, heads, head, 0, unroll=2)

    def part(j):
        return pltpu.make_async_remote_copy(
            src_ref=part_send.at[j - 1], dst_ref=part_recv.at[j - 1],
            send_sem=part_ss.at[j - 1], recv_sem=part_rs.at[j - 1],
            device_id=on(mate, tp), device_id_type=MESH,
        )

    def run(j):
        return pltpu.make_async_remote_copy(
            src_ref=run_send.at[j], dst_ref=run_recv.at[j],
            send_sem=run_ss.at[j], recv_sem=run_rs.at[j],
            device_id=on(prv, tp), device_id_type=MESH,
        )

    def add_part(j):
        part(j).wait_recv()
        dkv[...] += part_recv[j - 1].astype(F32)

    for j in range(HOPS, -1, -1):
        if j > 0:
            bwd_block(j, 2 * j - 1, j == HOPS)
            part_send[j - 1] = dkv[...].astype(BF16)
            part(j).start()
        bwd_block(j, 2 * j, False)
        if j < HOPS:
            @pl.when(core == 0)
            def _():
                add_part(j + 1)
        if j > 0:
            @pl.when(core == 1)
            def _():
                add_part(j)
        if j < HOPS:
            run(j).wait_recv()
            dkv[...] += run_recv[j].astype(F32)
        if j > 0:
            run_send[j - 1] = dkv[...].astype(BF16)
            run(j - 1).start()
        if j == 3:
            pass_on(1, 0)
        if j == 1:
            pass_on(1, 1)

    dkv_out[0] = (dkv[0] * score_scale).astype(BF16)
    dkv_out[1] = dkv[1].astype(BF16)
    outs = [
        pltpu.make_async_copy(dkv_out.at[0], dk_hbm, out_sem.at[0]),
        pltpu.make_async_copy(dkv_out.at[1], dv_hbm, out_sem.at[1]),
    ]
    for copy in outs:
        copy.start()
    for h in range(heads):
        dq_out[h] = (dq_t[h] * score_scale).T.astype(BF16)
        copy = pltpu.make_async_copy(dq_out.at[h], dq_hbm.at[:, pl.ds(h * width, width)], out_sem.at[2 + h])
        copy.start()
        outs.append(copy)
    for c in range(CHUNKS):
        own_out[c] = mm(attn[...], w_v[0, :, c * cols : (c + 1) * cols]).astype(BF16)
    for i in range(2):
        for way in range(2):
            c = 2 * way + i
            x_pass(1, way, i).wait_recv()
            own_out[c] = (own_out[c].astype(F32) + rs_recv[c].astype(F32)).astype(BF16)
            copy = pltpu.make_async_copy(
                own_out.at[c], out_hbm.at[:, pl.ds(c * cols, cols)], out_sem.at[2 + heads + c]
            )
            copy.start()
            outs.append(copy)

    for j in range(1, HOPS + 1):
        for i in range(2):
            hop(j, i).wait_send()
            from_mate(j, i).wait_send()
        part(j).wait_send()
        run(j - 1).wait_send()
    for ph in range(2):
        for c in range(CHUNKS):
            x_own(ph, c, own_src(ph, c)).wait_send()
            x_pass(ph, c // 2, c % 2).wait_send()
    for copy in outs:
        copy.wait()


def body(ctx_size, queries, keys, values, out_weight, cotangent, doc_lengths):
    tok = queries.shape[0]
    heads = queries.shape[1] // HEAD_WIDTH
    half = cotangent.shape[1]
    cols = half // CHUNKS
    width = HEAD_WIDTH
    slots = 2 * HOPS + 1
    any_spec = pl.BlockSpec(memory_space=pl.ANY)
    vmem = pltpu.VMEM
    dma = pltpu.SemaphoreType.DMA
    scratch = [
        vmem((heads, tok, width), BF16),
        vmem((heads, width, tok), BF16),
        vmem((slots, 2, tok, width), BF16),
        vmem((slots, width, tok), BF16),
        vmem((slots, width, tok), BF16),
        vmem((2, heads * width, half), BF16),
        vmem((2, CHUNKS, tok, cols), BF16),
        vmem((slots, heads, tok, tok), F32),
        vmem((2, tok, tok), F32),
        vmem((heads, width, tok), F32),
        vmem((heads, width, tok), BF16),
        vmem((tok, heads * width), BF16),
        vmem((heads, 1, tok), F32),
        vmem((heads, 1, tok), F32),
        vmem((HOPS + 1, heads, 1, tok), F32),
        vmem((heads, 1, tok), F32),
        vmem((heads * width, tok), F32),
        vmem((heads, width, tok), BF16),
        vmem((heads, tok, width), BF16),
        vmem((heads, width, tok), F32),
        vmem((2, tok, width), F32),
        vmem((HOPS, 2, tok, width), BF16),
        vmem((HOPS, 2, tok, width), BF16),
        vmem((HOPS, 2, tok, width), BF16),
        vmem((HOPS, 2, tok, width), BF16),
        vmem((2, 2, CHUNKS // 2, tok, cols), BF16),
        vmem((CHUNKS, tok, cols), BF16),
        vmem((CHUNKS, tok, cols), BF16),
        vmem((CHUNKS, tok, cols), BF16),
        vmem((heads, tok, width), BF16),
        vmem((2, tok, width), BF16),
        dma((2 + heads + CHUNKS,)),
        dma((2,)),
        dma((2 + heads + CHUNKS,)),
        dma((HOPS, 2)), dma((HOPS, 2)),
        dma((HOPS, 2)), dma((HOPS, 2)),
        dma((2, 2, CHUNKS // 2)), dma((2, 2, CHUNKS // 2)),
        dma((2, 2, CHUNKS // 2)), dma((2, 2, CHUNKS // 2)),
        dma((HOPS,)), dma((HOPS,)),
        dma((HOPS,)), dma((HOPS,)),
    ]
    return pl.pallas_call(
        partial(kernel, ctx_size),
        out_shape=(
            jax.ShapeDtypeStruct((tok, half), BF16),
            jax.ShapeDtypeStruct((tok, heads * width), BF16),
            jax.ShapeDtypeStruct((tok, width), BF16),
            jax.ShapeDtypeStruct((tok, width), BF16),
        ),
        in_specs=[any_spec] * 5 + [pl.BlockSpec(memory_space=pltpu.VMEM)],
        out_specs=[any_spec] * 4,
        scratch_shapes=scratch,
        compiler_params=pltpu.CompilerParams(
            collective_id=0, has_side_effects=True, vmem_limit_bytes=60 * 1024 * 1024
        ),
    )(queries, keys, values, out_weight, cotangent, doc_lengths.reshape(1, -1))


def solution(mesh):
    in_specs = (P("ctx", "tp"), P("ctx", "tp"), P("ctx", "tp"), P("tp", None), P("ctx", "tp"), P())
    out_specs = (P("ctx", "tp"), P("ctx", "tp"), P("ctx", "tp"), P("ctx", "tp"))
    return jax.shard_map(
        partial(body, mesh.shape["ctx"]), mesh=mesh, in_specs=in_specs, out_specs=out_specs, check_vma=False
    )
```

profile of v0, /device:TPU:24, one launch (start us, length us, event | category | flops | bytes accessed | tf_op | source)
XLA Modules:
  0.0 81.6 jit_solution(14591905896508892739)
XLA Ops:
  0.6 73.9 %shard_map.93 = (bf16[256,2048]{1,0:T(8,128)(2,1)}, bf16[256,1024]{1,0:T(8,128)(2,1)}, bf16[256,128]{1,0:T(8,128)(2,1)}, bf16[256,128]{1,0:T(8,128)(2,1)}) custom-call(bf16[256,1024]{1,0:T(8,128)(2,1)} %q_hbm.1, bf16[256,128]{1,0:T(8,128)(2,1)} %k_hbm.1, bf16[256,128]{1,0:T(8,128)(2,1)} %v_hbm.1, bf16[1024,4096]{1,0:T(8,128)(2,1)} %w_hbm.1, ...), custom_call_target="tpu_custom_call" | custom-call | tf_op jit(solution)/shard_map/pallas_call | solution.py:419
  74.5 2.3 %copy.14 = bf16[256,2048]{1,0:T(8,128)(2,1)} copy(bf16[256,2048]{1,0:T(8,128)(2,1)} %get-tuple-element.8) | data formatting | bytes 2097152
  76.8 1.9 %copy.15 = bf16[256,1024]{1,0:T(8,128)(2,1)} copy(bf16[256,1024]{1,0:T(8,128)(2,1)} %get-tuple-element.9) | data formatting | bytes 1048576
  78.7 1.5 %copy.16 = bf16[256,128]{1,0:T(8,128)(2,1)} copy(bf16[256,128]{1,0:T(8,128)(2,1)} %get-tuple-element.10) | data formatting | bytes 131072
  80.2 1.5 %copy.17 = bf16[256,128]{1,0:T(8,128)(2,1)} copy(bf16[256,128]{1,0:T(8,128)(2,1)} %get-tuple-element.11) | data formatting | bytes 131072
where the time goes:
time: 82 us; the launch traced here: 81.6 us
  Pallas kernels  73.9 us (90%)
  local copies, waits for them, and re-layouts  7.12 us (9%)
    pallas_call x1, Pallas kernels, body(): pl.pallas_call(partial(kernel, ctx_size), out_shape=(jax.ShapeDtypeStruct...  73.9 us
    unnamed x4, local copies, waits for them, and re-layouts  7.12 us

commit v1 on v0

v1 whole, which is shorter than its diff:
```python
from functools import partial
import math

import jax
import jax.numpy as jnp
from jax import lax
from jax.experimental import pallas as pl
from jax.experimental.pallas import tpu as pltpu
from jax.sharding import PartitionSpec as P

HEAD_WIDTH = 128
HOPS = 4
CHUNKS = 4
W_PIECES = 4
NEG = -1e30
MESH = pl.DeviceIdType.MESH
F32 = jnp.float32
BF16 = jnp.bfloat16


def mm(a, b):
    return jnp.dot(a, b, preferred_element_type=F32)


def mm_nt(a, b):
    return lax.dot_general(a, b, (((1,), (1,)), ((), ())), preferred_element_type=F32)


def kernel(
    ctx_size,
    q_hbm, k_hbm, v_hbm, w_hbm, cot_hbm, lens_ref,
    own_out, dq_out, dk_out, dv_out,
    q_s, q_t, kv, k_t, v_t, v_pair, w_v, cot, exps, bias, o_t, o_low, attn,
    row_max, row_sum, stage_max, delta, ga_t, do_t, do_s, dq_t, dkv,
    part_send, part_recv, run_send, run_recv, relay, rs_send, rs_recv, prob_low, grad_low,
    load_sem, w_sem,
    hop_send, hop_recv, chip_send, chip_recv,
    x_send, x_recv, y_send, y_recv,
    part_ss, part_rs, run_ss, run_rs,
):
    heads, tok, width = q_s.shape
    half = own_out.shape[1]
    cols = half // CHUNKS
    me = lax.axis_index("ctx")
    tp = lax.axis_index("tp")
    core = lax.rem(me, 2)
    chip = me // 2
    chips = ctx_size // 2
    nxt = lax.rem(chip + 1, chips) * 2 + core
    prv = lax.rem(chip + chips - 1, chips) * 2 + core
    mate = me + 1 - 2 * core
    across = lax.rem(me + ctx_size // 2, ctx_size)
    score_scale = 1.0 / math.sqrt(HEAD_WIDTH)
    log2_scale = score_scale / math.log(2.0)

    def on(ctx_id, tp_id):
        return {"ctx": ctx_id, "tp": tp_id}

    kv_loads = [
        pltpu.make_async_copy(k_hbm, kv.at[0, 0], load_sem.at[0]),
        pltpu.make_async_copy(v_hbm, kv.at[0, 1], load_sem.at[1]),
    ]
    q_loads = [
        pltpu.make_async_copy(q_hbm.at[:, pl.ds(h * width, width)], q_s.at[h], load_sem.at[2 + h])
        for h in range(heads)
    ]
    cot_loads = [
        pltpu.make_async_copy(
            cot_hbm.at[:, pl.ds(c * cols, cols)], cot.at[0, :, pl.ds(c * cols, cols)], load_sem.at[2 + heads + c]
        )
        for c in range(CHUNKS)
    ]
    w_rows = heads * width // W_PIECES
    w_loads = [
        pltpu.make_async_copy(
            w_hbm.at[pl.ds(r * w_rows, w_rows), pl.ds(pl.multiple_of(side * half, half), half)],
            w_v.at[s, pl.ds(r * w_rows, w_rows)],
            w_sem.at[s, r],
        )
        for s, side in ((1, 1 - tp), (0, tp))
        for r in range(W_PIECES)
    ]
    for copy in kv_loads + q_loads:
        copy.start()

    barrier = pltpu.get_barrier_semaphore()
    friends = [(nxt, tp), (prv, tp), (mate, tp), (across, tp), (across, 1 - tp)]
    for friend in friends:
        pl.semaphore_signal(barrier, inc=1, device_id=on(*friend), device_id_type=MESH)
    pl.semaphore_wait(barrier, len(friends))

    def hop(j, i):
        src = (k_hbm, v_hbm)[i] if isinstance(j, int) and j == 1 else kv.at[2 * (j - 1), i]
        return pltpu.make_async_remote_copy(
            src_ref=src, dst_ref=kv.at[2 * j, i],
            send_sem=hop_send.at[j - 1, i], recv_sem=hop_recv.at[j - 1, i],
            device_id=on(nxt, tp), device_id_type=MESH,
        )

    def to_mate(j, i):
        turn = j - core
        return pltpu.make_async_remote_copy(
            src_ref=kv.at[2 * j, i], dst_ref=kv.at[2 * turn + 1, i],
            send_sem=chip_send.at[turn, i], recv_sem=chip_recv.at[turn, i],
            device_id=on(mate, tp), device_id_type=MESH,
        )

    def from_mate(j, i):
        return pltpu.make_async_remote_copy(
            src_ref=kv.at[2 * (j - 1), i], dst_ref=kv.at[2 * j - 1, i],
            send_sem=chip_send.at[j - 1, i], recv_sem=chip_recv.at[j - 1, i],
            device_id=on(mate, tp), device_id_type=MESH,
        )

    def first_hop():
        for i in range(2):
            hop(1, i).start()
            kv_loads[i].wait()

            @pl.when(core == 0)
            def _():
                to_mate(0, i).start()

    def forward_hop(j):
        for i in range(2):
            hop(j, i).wait_recv()

            @pl.when(j < HOPS)
            def _():
                hop(j + 1, i).start()

            @pl.when((j < HOPS) | (core == 1))
            def _():
                to_mate(j, i).start()

    def x_own(ph, c, src):
        way, i = c // 2, c % 2
        return pltpu.make_async_remote_copy(
            src_ref=src, dst_ref=relay.at[ph, way, i],
            send_sem=x_send.at[ph, way, i], recv_sem=x_recv.at[ph, way, i],
            device_id=on(across, tp if way == 0 else 1 - tp), device_id_type=MESH,
        )

    def x_pass(ph, way, i):
        c = 2 * way + i
        dst = cot.at[1, :, pl.ds(c * cols, cols)] if ph == 0 else rs_recv.at[c]
        return pltpu.make_async_remote_copy(
            src_ref=relay.at[ph, way, i], dst_ref=dst,
            send_sem=y_send.at[ph, way, i], recv_sem=y_recv.at[ph, way, i],
            device_id=on(across, 1 - tp if way == 0 else tp), device_id_type=MESH,
        )

    def own_src(ph, c):
        return cot_hbm.at[:, pl.ds(c * cols, cols)] if ph == 0 else rs_send.at[c]

    def pass_on(ph, i):
        for way in range(2):
            x_own(ph, 2 * way + i, own_src(ph, 2 * way + i)).wait_recv()
            x_pass(ph, way, i).start()

    first_hop()
    for c in (0, 2, 1, 3):
        x_own(0, c, own_src(0, c)).start()
    for copy in w_loads + cot_loads:
        copy.start()

    docs = lens_ref.shape[1]
    lens = jnp.broadcast_to(lens_ref[...].astype(F32), (docs, docs))
    before = lax.broadcasted_iota(jnp.int32, (docs, docs), 1) < lax.broadcasted_iota(
        jnp.int32, (docs, docs), 0
    )
    doc_start = jnp.sum(jnp.where(before, lens, 0.0), axis=1, keepdims=True)
    first = (me * tok).astype(F32)
    pos = lax.broadcasted_iota(jnp.int32, (1, tok), 1).astype(F32) + first
    start = jnp.max(jnp.where(doc_start <= pos, doc_start, 0.0), axis=0, keepdims=True) - first
    key_row = lax.broadcasted_iota(jnp.int32, (tok, tok), 0)
    query_col = lax.broadcasted_iota(jnp.int32, (tok, tok), 1)

    def set_bias(slot, d):
        allowed = key_row.astype(F32) >= start + jnp.asarray(d * tok, jnp.int32).astype(F32)
        if isinstance(d, int) and d == 0:
            allowed = allowed & (key_row <= query_col)
        bias[slot] = jnp.where(allowed, 0.0, NEG)

    def fwd_stage(stage, blocks):
        for slot, d in enumerate(blocks):
            k_t[d] = kv[d, 0].T
            turned = kv[d, 1].T
            if len(blocks) == 1:
                v_t[...] = turned
            else:
                v_pair[:, slot * tok : (slot + 1) * tok] = turned
            set_bias(slot, d)

        initial = isinstance(stage, int)
        for h in range(heads):
            scores = [mm(kv[d, 0], q_t[h]) * log2_scale + bias[slot] for slot, d in enumerate(blocks)]
            top = scores[0] if initial else jnp.maximum(scores[0], scores[1])
            top = jnp.max(top, axis=0, keepdims=True)
            if not initial:
                top = jnp.maximum(row_max[h], top)
            mass = None
            low = []
            for d, s in zip(blocks, scores):
                e = jnp.exp2(s - top)
                exps[d, h] = e
                mass = e if mass is None else mass + e
                low.append(e.astype(BF16))
            if initial:
                acc = mm(v_t[...], low[0])
            else:
                acc = mm(v_pair[...], jnp.concatenate(low, axis=0))
            mass = jnp.sum(mass, axis=0, keepdims=True)
            if not initial:
                shrink = jnp.exp2(row_max[h] - top)
                mass = mass + row_sum[h] * shrink
                acc = acc + o_t[h] * shrink
            row_max[h] = top
            row_sum[h] = mass
            stage_max[stage, h] = top
            o_t[h] = acc

    def grad_half(s):
        step = 4 * width
        for r in range(0, heads * width, step):
            term = mm_nt(w_v[s, r : r + step], cot[s])
            ga_t[r : r + step] = ga_t[r : r + step] + term if s else term

    for copy in q_loads:
        copy.wait()
    for h in range(heads):
        q_t[h] = q_s[h].T
    fwd_stage(0, [0])

    def forward_step(j, _):
        forward_hop(j)
        for i in range(2):
            from_mate(j, i).wait_recv()
        fwd_stage(j, [2 * j - 1, 2 * j])

        @pl.when(j == 2)
        def _():
            pass_on(0, 0)

        @pl.when(j == HOPS)
        def _():
            pass_on(0, 1)

        return 0

    lax.fori_loop(1, HOPS + 1, forward_step, 0)

    for h in range(heads):
        inverse = 1.0 / row_sum[h]
        low = (o_t[h] * inverse).astype(BF16)
        o_low[h] = low
        attn[:, h * width : (h + 1) * width] = low.T
        for stage in range(HOPS + 1):
            stage_max[stage, h] = jnp.exp2(stage_max[stage, h] - row_max[h]) * inverse
    for copy in w_loads[:W_PIECES]:
        copy.wait()
    for c in (0, 2, 1, 3):
        rs_send[c] = mm(attn[...], w_v[1, :, c * cols : (c + 1) * cols]).astype(BF16)
        x_own(1, c, rs_send.at[c]).start()

    for copy in w_loads[W_PIECES:] + cot_loads:
        copy.wait()
    grad_half(0)
    for way in range(2):
        for i in range(2):
            x_pass(0, way, i).wait_recv()
    grad_half(1)
    for h in range(heads):
        low = ga_t[h * width : (h + 1) * width].astype(BF16)
        do_t[h] = low
        do_s[h] = low.T
        delta[h] = jnp.sum(low.astype(F32) * o_low[h].astype(F32), axis=0, keepdims=True)

    dq_t[...] = jnp.zeros_like(dq_t)

    def bwd_block(stage, d, slot):
        rows = slice(slot * tok, (slot + 1) * tok)
        for h in range(heads):
            prob = exps[d, h] * stage_max[stage, h]
            grad = prob * (mm(kv[d, 1], do_t[h]) - delta[h])
            prob_low[:, h * tok : (h + 1) * tok] = prob.astype(BF16)
            grad_low[rows, h * tok : (h + 1) * tok] = grad.astype(BF16)
        dkv[1] = mm(prob_low[...], do_s[...].reshape(heads * tok, width))
        dkv[0] = mm(grad_low[rows], q_s[...].reshape(heads * tok, width))

    def add_dq(keys_turned, rows):
        for h in range(heads):
            dq_t[h] += mm(keys_turned, grad_low[:rows, h * tok : (h + 1) * tok])

    def part(j):
        return pltpu.make_async_remote_copy(
            src_ref=part_send.at[j - 1], dst_ref=part_recv.at[j - 1],
            send_sem=part_ss.at[j - 1], recv_sem=part_rs.at[j - 1],
            device_id=on(mate, tp), device_id_type=MESH,
        )

    def run(j):
        return pltpu.make_async_remote_copy(
            src_ref=run_send.at[j], dst_ref=run_recv.at[j],
            send_sem=run_ss.at[j], recv_sem=run_rs.at[j],
            device_id=on(prv, tp), device_id_type=MESH,
        )

    def add_part(j):
        part(j).wait_recv()
        dkv[...] += part_recv[j - 1].astype(F32)

    def run_on(j):
        run(j).wait_recv()
        dkv[...] += run_recv[j].astype(F32)

    def backward_step(it, _):
        j = HOPS - it
        bwd_block(j, 2 * j - 1, 0)
        part_send[j - 1] = dkv[...].astype(BF16)
        part(j).start()
        bwd_block(j, 2 * j, 1)
        add_dq(jnp.concatenate([k_t[2 * j - 1], k_t[2 * j]], axis=1), 2 * tok)

        @pl.when((core == 0) & (j < HOPS))
        def _():
            add_part(j + 1)

        @pl.when(core == 1)
        def _():
            add_part(j)

        @pl.when(j < HOPS)
        def _():
            run_on(j)

        run_send[j - 1] = dkv[...].astype(BF16)
        run(j - 1).start()

        @pl.when(j == 3)
        def _():
            pass_on(1, 0)

        @pl.when(j == 1)
        def _():
            pass_on(1, 1)

        return 0

    lax.fori_loop(0, HOPS, backward_step, 0)
    bwd_block(0, 0, 0)
    add_dq(k_t[0], tok)
    for h in range(heads):
        dq_out[:, h * width : (h + 1) * width] = (dq_t[h] * score_scale).T.astype(BF16)
    for c in range(CHUNKS):
        own_out[:, c * cols : (c + 1) * cols] = mm(attn[...], w_v[0, :, c * cols : (c + 1) * cols]).astype(BF16)

    @pl.when(core == 0)
    def _():
        add_part(1)

    run_on(0)
    dk_out[...] = (dkv[0] * score_scale).astype(BF16)
    dv_out[...] = dkv[1].astype(BF16)
    for i in range(2):
        for way in range(2):
            c = 2 * way + i
            x_pass(1, way, i).wait_recv()
            at = slice(c * cols, (c + 1) * cols)
            own_out[:, at] = (own_out[:, at].astype(F32) + rs_recv[c].astype(F32)).astype(BF16)

    for j in range(1, HOPS + 1):
        for i in range(2):
            hop(j, i).wait_send()
            from_mate(j, i).wait_send()
        part(j).wait_send()
        run(j - 1).wait_send()
    for ph in range(2):
        for c in range(CHUNKS):
            x_own(ph, c, own_src(ph, c)).wait_send()
            x_pass(ph, c // 2, c % 2).wait_send()


def body(ctx_size, queries, keys, values, out_weight, cotangent, doc_lengths):
    tok = queries.shape[0]
    heads = queries.shape[1] // HEAD_WIDTH
    half = cotangent.shape[1]
    cols = half // CHUNKS
    width = HEAD_WIDTH
    slots = 2 * HOPS + 1
    any_spec = pl.BlockSpec(memory_space=pl.ANY)
    vmem = pltpu.VMEM
    dma = pltpu.SemaphoreType.DMA
    scratch = [
        vmem((heads, tok, width), BF16),
        vmem((heads, width, tok), BF16),
        vmem((slots, 2, tok, width), BF16),
        vmem((slots, width, tok), BF16),
        vmem((width, tok), BF16),
        vmem((width, 2 * tok), BF16),
        vmem((2, heads * width, half), BF16),
        vmem((2, tok, half), BF16),
        vmem((slots, heads, tok, tok), F32),
        vmem((2, tok, tok), F32),
        vmem((heads, width, tok), F32),
        vmem((heads, width, tok), BF16),
        vmem((tok, heads * width), BF16),
        vmem((heads, 1, tok), F32),
        vmem((heads, 1, tok), F32),
        vmem((HOPS + 1, heads, 1, tok), F32),
        vmem((heads, 1, tok), F32),
        vmem((heads * width, tok), F32),
        vmem((heads, width, tok), BF16),
        vmem((heads, tok, width), BF16),
        vmem((heads, width, tok), F32),
        vmem((2, tok, width), F32),
        vmem((HOPS, 2, tok, width), BF16),
        vmem((HOPS, 2, tok, width), BF16),
        vmem((HOPS, 2, tok, width), BF16),
        vmem((HOPS, 2, tok, width), BF16),
        vmem((2, 2, CHUNKS // 2, tok, cols), BF16),
        vmem((CHUNKS, tok, cols), BF16),
        vmem((CHUNKS, tok, cols), BF16),
        vmem((tok, heads * tok), BF16),
        vmem((2 * tok, heads * tok), BF16),
        dma((2 + heads + CHUNKS,)),
        dma((2, W_PIECES)),
        dma((HOPS, 2)), dma((HOPS, 2)),
        dma((HOPS, 2)), dma((HOPS, 2)),
        dma((2, 2, CHUNKS // 2)), dma((2, 2, CHUNKS // 2)),
        dma((2, 2, CHUNKS // 2)), dma((2, 2, CHUNKS // 2)),
        dma((HOPS,)), dma((HOPS,)),
        dma((HOPS,)), dma((HOPS,)),
    ]
    shapes = [(tok, half), (tok, heads * width), (tok, width), (tok, width)]
    results = pl.pallas_call(
        partial(kernel, ctx_size),
        out_shape=tuple(pltpu.VMEM(shape, BF16) for shape in shapes),
        in_specs=[any_spec] * 5 + [pl.BlockSpec(memory_space=pltpu.VMEM)],
        out_specs=[pl.BlockSpec(memory_space=pltpu.VMEM)] * 4,
        scratch_shapes=scratch,
        compiler_params=pltpu.CompilerParams(
            collective_id=0, has_side_effects=True, vmem_limit_bytes=60 * 1024 * 1024
        ),
    )(queries, keys, values, out_weight, cotangent, doc_lengths.reshape(1, -1))
    return pl.pallas_call(
        write_out,
        out_shape=tuple(jax.ShapeDtypeStruct(shape, BF16) for shape in shapes),
        in_specs=[pl.BlockSpec(memory_space=pltpu.VMEM)] * 4,
        out_specs=[any_spec] * 4,
        scratch_shapes=[dma((4,))],
    )(*[pltpu.with_memory_space_constraint(result, pltpu.VMEM) for result in results])


def write_out(*refs):
    sources, targets, sem = refs[:4], refs[4:8], refs[8]
    copies = [pltpu.make_async_copy(a, b, sem.at[i]) for i, (a, b) in enumerate(zip(sources, targets))]
    for copy in copies:
        copy.start()
    for copy in copies:
        copy.wait()


def solution(mesh):
    in_specs = (P("ctx", "tp"), P("ctx", "tp"), P("ctx", "tp"), P("tp", None), P("ctx", "tp"), P())
    out_specs = (P("ctx", "tp"), P("ctx", "tp"), P("ctx", "tp"), P("ctx", "tp"))
    return jax.shard_map(
        partial(body, mesh.shape["ctx"]), mesh=mesh, in_specs=in_specs, out_specs=out_specs, check_vma=False
    )
```

time: 82 us -> 68.1 us (0.83)
  local copies, waits for them, and re-layouts: 7.12 us -> 0 us
  Pallas kernels: 73.9 us -> 67.4 us
    unnamed x4 -> x0, local copies, waits for them, and re-layouts: 7.12 us -> none
    pallas_call x1 -> x2, Pallas kernels: 73.9 us -> 67.4 us  [the longest x1 66.2 us: body(): pl.pallas_call(partial(kernel, ctx_size), out_shape=tuple((pltpu.VMEM(sha...]
where the time goes in v1:
time: 68.1 us; the launch traced here: 68 us
  Pallas kernels  67.4 us (99%)
    pallas_call x1, Pallas kernels, body(): pl.pallas_call(partial(kernel, ctx_size), out_shape=tuple((pltpu.VMEM(sha...  66.2 us

profile of v1, /device:TPU:24, one launch (start us, length us, event | category | flops | bytes accessed | tf_op | source)
XLA Modules:
  0.0 68.0 jit_solution(11006968139290058398)
XLA Ops:
  0.6 66.2 %shard_map.93 = (bf16[256,2048]{1,0:T(8,128)(2,1)S(1)}, bf16[256,1024]{1,0:T(8,128)(2,1)S(1)}, bf16[256,128]{1,0:T(8,128)(2,1)S(1)}, bf16[256,128]{1,0:T(8,128)(2,1)S(1)}) custom-call(bf16[256,1024]{1,0:T(8,128)(2,1)} %q_hbm.1, bf16[256,128]{1,0:T(8,128)(2,1)} %k_hbm.1, bf16[256,128]{1,0:T(8,128)(2,1)} %v_hbm.1, bf16[1024,4096]{1,0:T(8,128)(2,1)} %w_hbm.1, ...), custom_call_target="tpu_custom_call" | custom-call | tf_op jit(solution)/shard_map/pallas_call | solution.py:436
  66.8 1.2 %shard_map.94 = (bf16[256,2048]{1,0:T(8,128)(2,1)}, bf16[256,1024]{1,0:T(8,128)(2,1)}, bf16[256,128]{1,0:T(8,128)(2,1)}, bf16[256,128]{1,0:T(8,128)(2,1)}) custom-call(bf16[256,2048]{1,0:T(8,128)(2,1)S(1)} %get-tuple-element.8.refs_0_, bf16[256,1024]{1,0:T(8,128)(2,1)S(1)} %get-tuple-element.9.refs_1_, bf16[256,128]{1,0:T(8,128)(2,1)S(1)} %get-tuple-element.10.refs_2_, ...), custom_call_target="tpu_custom_call" | custom-call | tf_op jit(solution)/shard_map/pallas_call | solution.py:446

commit v2 on v1

--- a/solution.py
+++ b/solution.py
@@ -12,6 +12,7 @@
 HOPS = 4
 CHUNKS = 4
 W_PIECES = 4
+PIECE = 128
 NEG = -1e30
 MESH = pl.DeviceIdType.MESH
 F32 = jnp.float32
@@ -33,6 +34,7 @@
     q_s, q_t, kv, k_t, v_t, v_pair, w_v, cot, exps, bias, o_t, o_low, attn,
     row_max, row_sum, stage_max, delta, ga_t, do_t, do_s, dq_t, dkv,
     part_send, part_recv, run_send, run_recv, relay, rs_send, rs_recv, prob_low, grad_low,
+    score_buf, exp_low,
     load_sem, w_sem,
     hop_send, hop_recv, chip_send, chip_recv,
     x_send, x_recv, y_send, y_recv,
@@ -193,23 +195,39 @@
             set_bias(slot, d)
 
         initial = isinstance(stage, int)
+        pieces = [(slot, d, r) for slot, d in enumerate(blocks) for r in range(0, tok, PIECE)]
+
+        def score_piece(h, piece, top):
+            slot, d, r = piece
+            s = mm(kv[d, 0, r : r + PIECE], q_t[h]) * log2_scale + bias[slot, r : r + PIECE]
+            score_buf[h % 2, slot, r : r + PIECE] = s
+            part_top = jnp.max(s.reshape(PIECE // 8, 8, tok), axis=0)
+            return part_top if top is None else jnp.maximum(top, part_top)
+
+        def exp_piece(h, piece, top, mass):
+            slot, d, r = piece
+            e = jnp.exp2(score_buf[h % 2, slot, r : r + PIECE] - top)
+            exps[d, h, r : r + PIECE] = e
+            exp_low[h % 2, slot * tok + r : slot * tok + r + PIECE] = e.astype(BF16)
+            part_mass = jnp.sum(e.reshape(PIECE // 8, 8, tok), axis=0)
+            return part_mass if mass is None else mass + part_mass
+
+        coming = None
+        for piece in pieces:
+            coming = score_piece(0, piece, coming)
         for h in range(heads):
-            scores = [mm(kv[d, 0], q_t[h]) * log2_scale + bias[slot] for slot, d in enumerate(blocks)]
-            top = scores[0] if initial else jnp.maximum(scores[0], scores[1])
-            top = jnp.max(top, axis=0, keepdims=True)
+            top = jnp.max(coming, axis=0, keepdims=True)
             if not initial:
                 top = jnp.maximum(row_max[h], top)
-            mass = None
-            low = []
-            for d, s in zip(blocks, scores):
-                e = jnp.exp2(s - top)
-                exps[d, h] = e
-                mass = e if mass is None else mass + e
-                low.append(e.astype(BF16))
+            coming, mass = None, None
+            for piece in pieces:
+                if h + 1 < heads:
+                    coming = score_piece(h + 1, piece, coming)
+                mass = exp_piece(h, piece, top, mass)
             if initial:
-                acc = mm(v_t[...], low[0])
+                acc = mm(v_t[...], exp_low[h % 2, :tok])
             else:
-                acc = mm(v_pair[...], jnp.concatenate(low, axis=0))
+                acc = mm(v_pair[...], exp_low[h % 2])
             mass = jnp.sum(mass, axis=0, keepdims=True)
             if not initial:
                 shrink = jnp.exp2(row_max[h] - top)
@@ -423,6 +441,8 @@
         vmem((CHUNKS, tok, cols), BF16),
         vmem((tok, heads * tok), BF16),
         vmem((2 * tok, heads * tok), BF16),
+        vmem((2, 2, tok, tok), F32),
+        vmem((2, 2 * tok, tok), BF16),
         dma((2 + heads + CHUNKS,)),
         dma((2, W_PIECES)),
         dma((HOPS, 2)), dma((HOPS, 2)),

time: 68.1 us -> 68.1 us (level)
  no operation moved by 1% of the time
where the time goes in v2:
time: 68.1 us; the launch traced here: 68 us
  Pallas kernels  67.4 us (99%)
    pallas_call x1, Pallas kernels, body(): pl.pallas_call(partial(kernel, ctx_size), out_shape=tuple((pltpu.VMEM(sha...  66.2 us

profile of v2, /device:TPU:24, one launch (start us, length us, event | category | flops | bytes accessed | tf_op | source)
XLA Modules:
  0.0 68.0 jit_solution(5646213955044821892)
XLA Ops:
  0.6 66.2 %shard_map.93 = (bf16[256,2048]{1,0:T(8,128)(2,1)S(1)}, bf16[256,1024]{1,0:T(8,128)(2,1)S(1)}, bf16[256,128]{1,0:T(8,128)(2,1)S(1)}, bf16[256,128]{1,0:T(8,128)(2,1)S(1)}) custom-call(bf16[256,1024]{1,0:T(8,128)(2,1)} %q_hbm.1, bf16[256,128]{1,0:T(8,128)(2,1)} %k_hbm.1, bf16[256,128]{1,0:T(8,128)(2,1)} %v_hbm.1, bf16[1024,4096]{1,0:T(8,128)(2,1)} %w_hbm.1, ...), custom_call_target="tpu_custom_call" | custom-call | tf_op jit(solution)/shard_map/pallas_call | solution.py:456
  66.8 1.2 %shard_map.94 = (bf16[256,2048]{1,0:T(8,128)(2,1)}, bf16[256,1024]{1,0:T(8,128)(2,1)}, bf16[256,128]{1,0:T(8,128)(2,1)}, bf16[256,128]{1,0:T(8,128)(2,1)}) custom-call(bf16[256,2048]{1,0:T(8,128)(2,1)S(1)} %get-tuple-element.8.refs_0_, bf16[256,1024]{1,0:T(8,128)(2,1)S(1)} %get-tuple-element.9.refs_1_, bf16[256,128]{1,0:T(8,128)(2,1)S(1)} %get-tuple-element.10.refs_2_, ...), custom_call_target="tpu_custom_call" | custom-call | tf_op jit(solution)/shard_map/pallas_call | solution.py:466

commit v3 on v2

--- a/solution.py
+++ b/solution.py
@@ -254,16 +254,16 @@
         forward_hop(j)
         for i in range(2):
             from_mate(j, i).wait_recv()
+
+        @pl.when(j == 2)
+        def _():
+            pass_on(0, 0)
+
+        @pl.when(j == HOPS)
+        def _():
+            pass_on(0, 1)
+
         fwd_stage(j, [2 * j - 1, 2 * j])
-
-        @pl.when(j == 2)
-        def _():
-            pass_on(0, 0)
-
-        @pl.when(j == HOPS)
-        def _():
-            pass_on(0, 1)
-
         return 0
 
     lax.fori_loop(1, HOPS + 1, forward_step, 0)
@@ -355,11 +355,11 @@
         run_send[j - 1] = dkv[...].astype(BF16)
         run(j - 1).start()
 
-        @pl.when(j == 3)
+        @pl.when(j == HOPS)
         def _():
             pass_on(1, 0)
 
-        @pl.when(j == 1)
+        @pl.when(j == 2)
         def _():
             pass_on(1, 1)
 

time: 68.1 us -> 68.1 us (level)
  no operation moved by 1% of the time
where the time goes in v3:
time: 68.1 us; the launch traced here: 68 us
  Pallas kernels  67.4 us (99%)
    pallas_call x1, Pallas kernels, body(): pl.pallas_call(partial(kernel, ctx_size), out_shape=tuple((pltpu.VMEM(sha...  66.2 us

profile of v3, /device:TPU:24, one launch (start us, length us, event | category | flops | bytes accessed | tf_op | source)
XLA Modules:
  0.0 68.0 jit_solution(9562744668148815706)
XLA Ops:
  0.6 66.2 %shard_map.93 = (bf16[256,2048]{1,0:T(8,128)(2,1)S(1)}, bf16[256,1024]{1,0:T(8,128)(2,1)S(1)}, bf16[256,128]{1,0:T(8,128)(2,1)S(1)}, bf16[256,128]{1,0:T(8,128)(2,1)S(1)}) custom-call(bf16[256,1024]{1,0:T(8,128)(2,1)} %q_hbm.1, bf16[256,128]{1,0:T(8,128)(2,1)} %k_hbm.1, bf16[256,128]{1,0:T(8,128)(2,1)} %v_hbm.1, bf16[1024,4096]{1,0:T(8,128)(2,1)} %w_hbm.1, ...), custom_call_target="tpu_custom_call" | custom-call | tf_op jit(solution)/shard_map/pallas_call | solution.py:456
  66.8 1.2 %shard_map.94 = (bf16[256,2048]{1,0:T(8,128)(2,1)}, bf16[256,1024]{1,0:T(8,128)(2,1)}, bf16[256,128]{1,0:T(8,128)(2,1)}, bf16[256,128]{1,0:T(8,128)(2,1)}) custom-call(bf16[256,2048]{1,0:T(8,128)(2,1)S(1)} %get-tuple-element.8.refs_0_, bf16[256,1024]{1,0:T(8,128)(2,1)S(1)} %get-tuple-element.9.refs_1_, bf16[256,128]{1,0:T(8,128)(2,1)S(1)} %get-tuple-element.10.refs_2_, ...), custom_call_target="tpu_custom_call" | custom-call | tf_op jit(solution)/shard_map/pallas_call | solution.py:466
